TPU v7x, 32 devices: a whole 2x2x4 slice. The times are simulated.
32 devices in a mesh: exp: 4 (over z), tile: 8 (over y, x, core).
Axes of the slice: x: 2, y: 2, z: 4, core: 2. Of those that a mesh axis runs over, the one named last changes fastest.
Arguments:
- science: bfloat16 [4, 8, 128, 256], P('exp', 'tile'), may hold values from -6 to 6
- mask_bits: int32 [4, 8, 128, 256], P('exp', 'tile'), may hold values from 0 to 1023, as said below
- variance: bfloat16 [4, 8, 128, 256], P('exp', 'tile'), may hold values from 0.25 to 4
- kernel_poly: float32 [4, 8, 8, 3], P('exp', 'tile'), may hold values from -5 to 5
- basis_rows: bfloat16 [8, 31], replicated, may hold values from -1 to 1
- basis_cols: bfloat16 [8, 31], replicated, may hold values from -1 to 1
- destination: int32 [4, 8, 16, 1], P('exp', 'tile'), may hold values from 0 to 7, as said below
- row_offset: int32 [4, 8, 16], P('exp', 'tile'), may hold values from 0 to 1023, as said below
Outputs:
- template: bfloat16 [8192, 128], P('tile')
- difference: bfloat16 [4, 8, 128, 256], P('exp', 'tile')
Inputs may be any that keep to these rules, and one draw needn't show every extreme that they name: `destination`: the pieces of the CCD region at tile index t land, in order of piece number, in contiguous runs on tiles t, t + 1 and t + 2 modulo 8; at most 8 pieces of one region land in one tile, and in every draw some region has exactly 8 in one tile. `row_offset`: offsets of consecutive rows of pieces mostly rise by about 16, wrapping within a tile. `mask_bits`: A pixel is rejected where any of bits 0, 1 or 2 is set; only bits 0 to 9 are used, and in every draw some pixel has all ten set.
All inputs are finite; a program needn't handle non-finite values.
Results may differ from a plain program's by a relative error of at most 0.0063.
Values may be sent and summed in bfloat16 or wider, within the bound.
No kernel may reach another device: no remote copies, remote signals or barrier semaphores. Data moves between devices by JAX's collectives and lax.ppermute only.
A program may use at most 64 MiB of HBM per device.

v0:
```python
import jax
import jax.numpy as jnp
from jax import lax
from jax.sharding import PartitionSpec as P

PR = 16
PC = 128
TR = 1024


def shifted(shard, axis, by):
    length = lax.axis_size(axis)
    return lax.ppermute(shard, axis, [(i, (i + by) % length) for i in range(length)])


def padded_2(cells, sides, width):
    for axis, dim in sides:
        count = lax.axis_size(axis)
        ends = count - 1
        head = lax.slice_in_dim(cells, 0, width, axis=dim)
        tail = lax.slice_in_dim(cells, cells.shape[dim] - width, cells.shape[dim], axis=dim)
        cells = jnp.concatenate(
            [
                lax.ppermute(tail, axis, [(i, (i + 1) % count) for i in range(ends)]),
                cells,
                lax.ppermute(head, axis, [((i + 1) % count, i) for i in range(ends)]),
            ],
            axis=dim,
        )
    return cells


def toeplitz(kernel_taps, length):
    half_width = kernel_taps.shape[1] // 2
    position = jnp.arange(length, dtype=jnp.int32)
    offset_index = position[:, None] - position[None, :] + half_width
    inside = (offset_index >= 0) & (offset_index < kernel_taps.shape[1])
    tap_index = jnp.where(inside, offset_index, 0)
    band_table = jnp.take(kernel_taps, tap_index, axis=1)
    return jnp.where(inside[None], band_table, jnp.zeros_like(band_table))


def coefficient_maps(kernel_terms, height, across):
    y_norm = (jnp.arange(height, dtype=jnp.int32).astype(jnp.float32) - (height - 1) / 2.0) / (
        height / 2.0
    )
    x_norm = (jnp.arange(across, dtype=jnp.int32).astype(jnp.float32) - (across - 1) / 2.0) / (
        across / 2.0
    )
    return (
        kernel_terms[:, 0, None, None]
        + kernel_terms[:, 1, None, None] * y_norm[None, :, None]
        + kernel_terms[:, 2, None, None] * x_norm[None, None, :]
    )


def send_along(bundle, step):
    return shifted((bundle[0], bundle[1], bundle[2]), "tile", step)


def send_back(bundle, step):
    return shifted(bundle, "tile", -step)


def body(
    science, mask_bits, variance, kernel_poly, basis_rows, basis_cols, destination, row_offset
):
    region = science[0, 0]
    height, across = region.shape
    col_band = toeplitz(basis_cols, across)
    row_band = toeplitz(basis_rows, height)
    first_pass = jnp.einsum(
        "yc,bcx->byx", region, col_band, preferred_element_type=jnp.float32
    ).astype(jnp.bfloat16)
    second_pass = jnp.einsum(
        "biy,bix->byx", row_band, first_pass, preferred_element_type=jnp.float32
    )
    matched = jnp.sum(coefficient_maps(kernel_poly[0, 0], height, across) * second_pass, axis=0)
    rejected = jnp.bitwise_and(mask_bits[0, 0], 7) != 0
    weight = jnp.where(rejected, jnp.float32(0.0), 1.0 / variance[0, 0].astype(jnp.float32))
    weighted = (matched * weight).astype(jnp.bfloat16)
    weight_sent = weight.astype(jnp.bfloat16)
    block_rows = height // PR
    block_cols = across // PC

    def to_pieces(picture):
        return (
            picture.reshape(block_rows, PR, block_cols, PC)
            .transpose(0, 2, 1, 3)
            .reshape(-1, PR, PC)
        )

    target = destination.reshape(-1)
    offset = row_offset.reshape(-1)
    pieces_count = target.shape[0]
    tile_count = lax.axis_size("tile")
    reach = 3
    slot_count = pieces_count // 2
    slot_total = reach * slot_count
    offset = jnp.where(target == tile_count - 1, jnp.minimum(offset, TR - PR), offset)
    relative = (target - lax.axis_index("tile") + tile_count) % tile_count
    one_hot = (relative[:, None] == jnp.arange(reach, dtype=jnp.int32)[None, :]).astype(jnp.int32)
    earlier = jnp.cumsum(one_hot, axis=0) - one_hot
    slot_rank = jnp.sum(earlier * one_hot, axis=1)
    send_index = relative * slot_count + slot_rank
    send_pixels = (
        jnp.zeros((slot_total, PR, PC), jnp.bfloat16).at[send_index].set(to_pieces(weighted))
    )
    send_weights = (
        jnp.zeros((slot_total, PR, PC), jnp.bfloat16).at[send_index].set(to_pieces(weight_sent))
    )
    send_offsets = jnp.full((slot_total,), -1, jnp.int32).at[send_index].set(offset)
    send_pixels = send_pixels.reshape(reach, slot_count, PR, PC)
    send_weights = send_weights.reshape(reach, slot_count, PR, PC)
    send_offsets = send_offsets.reshape(reach, slot_count)
    got_list = [(send_pixels[0], send_weights[0], send_offsets[0])]
    for step in range(1, reach):
        got_list.append(
            send_along((send_pixels[step], send_weights[step], send_offsets[step]), step)
        )
    got_pixels = jnp.stack([item[0] for item in got_list])
    got_weights = jnp.stack([item[1] for item in got_list])
    got_offsets = jnp.stack([item[2] for item in got_list])
    extent = TR + PR
    is_live = got_offsets >= 0
    sky_row = jnp.where(
        is_live[..., None], got_offsets[..., None] + jnp.arange(PR, dtype=jnp.int32), extent - 1
    ).reshape(-1)
    pixel_sum = (
        jnp.zeros((extent, PC), jnp.float32)
        .at[sky_row]
        .add(got_pixels.reshape(-1, PC).astype(jnp.float32))
    )
    weight_sum = (
        jnp.zeros((extent, PC), jnp.float32)
        .at[sky_row]
        .add(got_weights.reshape(-1, PC).astype(jnp.float32))
    )
    local_sums = jnp.stack([pixel_sum, weight_sum])[:, : extent - 1]
    rim_rows = PR - 1
    padded = padded_2(local_sums, (("tile", 1),), rim_rows)
    core_rows = padded[:, rim_rows : rim_rows + extent - 1]
    core_rows = core_rows.at[:, :rim_rows].add(padded[:, :rim_rows])
    core_rows = core_rows.at[:, TR : TR + rim_rows].add(padded[:, rim_rows + extent - 1 :])
    extended = jnp.concatenate([core_rows, jnp.zeros((2, 1, PC), jnp.float32)], axis=1)
    totals = lax.psum(extended, "exp")
    template_ext = (totals[0] / jnp.maximum(totals[1], 1.0)).astype(jnp.bfloat16)
    cutout = template_ext[sky_row].reshape(reach, slot_count, PR, PC)
    returned_list = [cutout[0]]
    for step in range(1, reach):
        returned_list.append(send_back(cutout[step], step))
    returned = jnp.stack(returned_list)
    own_cutouts = returned.reshape(slot_total, PR, PC)[send_index]
    back_image = (
        own_cutouts.reshape(block_rows, block_cols, PR, PC)
        .transpose(0, 2, 1, 3)
        .reshape(height, across)
    )
    difference = (matched - back_image.astype(jnp.float32)).astype(jnp.bfloat16)
    return (template_ext[:TR], difference[None, None])


def solution(mesh):
    placed = (
        P("exp", "tile", None, None),
        P("exp", "tile", None, None),
        P("exp", "tile", None, None),
        P("exp", "tile", None, None),
        P(),
        P(),
        P("exp", "tile", None, None),
        P("exp", "tile", None),
    )
    return jax.shard_map(
        body,
        mesh=mesh,
        in_specs=placed,
        out_specs=(P("tile", None), P("exp", "tile", None, None)),
        check_vma=False,
    )
```

profile of v0, /device:TPU:0, one launch (start us, length us, event | category | flops | bytes accessed | tf_op | source)
XLA Modules:
  0.0 417.3 jit_solution(487939907609007611)
XLA Ops:
  7.2 0.7 bitcast_select_fusion
  7.9 0.1 fusion.58
  8.0 0.2 select_reduce_fusion
  8.2 0.7 fusion.64
  8.9 0.6 scatter_custom_fusion
  9.6 0.5 collective-permute-start
  10.1 2.5 collective-permute-start.1
  12.6 0.1 fusion.32
  12.9 0.7 copy.30
  13.6 0.1 copy.28
  13.8 0.1 copy.22
  13.9 228.9 %gather_fusion.1 = bf16[65536,8]{1,0:T(8,128)(2,1)} fusion(bf16[8,31]{0,1:T(8,128)(2,1)S(1)} %copy.22, s32[65536]{0:T(1024)S(1)} %broadcast_clamp_fusion), kind=kCustom, calls=%fused_computation.1 | custom fusion | bytes 2359296 | tf_op jit(solution)/shard_map/jit(_take)/gather | solution.py:39
  242.8 15.9 %copy.23 = bf16[256,256,8]{0,1,2:T(8,128)(2,1)S(1)} copy(bf16[256,256,8]{2,1,0:T(8,128)(2,1)} %bitcast.92) | data formatting | bytes 2097152 | tf_op jit(solution)/shard_map/jit(_take)/gather | solution.py:39
  258.7 0.1 copy.20
  258.8 57.8 %gather_fusion = bf16[16384,8]{1,0:T(8,128)(2,1)} fusion(bf16[8,31]{0,1:T(8,128)(2,1)S(1)} %copy.20, s32[16384]{0:T(1024)S(1)} %fusion.44), kind=kCustom, calls=%fused_computation | custom fusion | bytes 589824 | tf_op jit(solution)/shard_map/jit(_take)/gather | solution.py:39
  316.6 6.3 %copy.21 = bf16[128,128,8]{0,1,2:T(8,128)(2,1)S(1)} copy(bf16[128,128,8]{2,1,0:T(8,128)(2,1)} %bitcast.99) | data formatting | bytes 524288 | tf_op jit(solution)/shard_map/jit(_take)/gather | solution.py:39
  323.1 0.8 fusion
  324.1 0.1 convert_bitcast_fusion.1
  324.3 1.0 scatter_fusion.1
  325.3 1.3 collective-permute-start.4
  326.6 1.5 collective-permute-start.5
  328.2 1.0 scatter_fusion
  329.2 0.1 collective-permute-start.2
  329.3 0.3 collective-permute-start.3
  329.7 0.1 add_select_fusion
  329.7 0.1 select_n.155
  329.9 1.6 collective-permute-done.5
  331.5 2.3 scatter_custom_fusion.4
  333.8 0.4 collective-permute-done.3
  334.2 2.3 scatter_custom_fusion.2
  336.5 1.8 collective-permute-start.6
  338.4 0.8 collective-permute-done.6
  339.2 1.3 collective-permute-start.7
  340.6 0.2 scatter-add.26
  340.8 1.5 collective-permute-done.7
  342.3 1.1 concatenate.11
  343.4 56.9 %all-reduce.3.cloned.1.call-done = f32[2,1040,128]{2,1,0:T(8,128)} async-done(((f32[2,1040,128]{2,1,0:T(8,128)}), f32[2,1040,128]{2,1,0:T(8,128)}) %all-reduce.3.cloned.1.call-update) | async-done | bytes 1064976 | tf_op jit(solution)/shard_map/psum | solution.py:146
  400.3 1.4 fusion.74
  401.6 1.4 gather_fusion.2
  403.1 2.0 collective-permute-start.8
  405.1 0.6 collective-permute-start.9
  405.6 0.1 fusion.13
  405.7 0.7 slice_bitcast_fusion
  406.5 0.4 collective-permute-done.8
  406.9 2.1 collective-permute-done.9
  409.0 0.6 gather_fusion.3
  409.7 0.1 reshape.546
  409.8 0.6 fusion.39
  (53 shorter events, 1.0 us)
Async XLA Ops:
  7.2 315.9 %copy-start = (bf16[1,1,128,256]{3,2,1,0:T(8,128)(2,1)S(1)}, bf16[1,1,128,256]{3,2,1,0:T(8,128)(2,1)}, u32[]{:S(2)}) copy-start(bf16[1,1,128,256]{3,2,1,0:T(8,128)(2,1)} %param.12) | copy-start | bytes 196612
  7.2 6.6 %copy-start.4 = (bf16[8,31]{1,0:T(8,128)(2,1)S(1)}, bf16[8,31]{1,0:T(8,128)(2,1)}, u32[]{:S(2)}) copy-start(bf16[8,31]{1,0:T(8,128)(2,1)} %param.17) | copy-start | bytes 1492
  7.2 393.1 %all-reduce.3.cloned.1.call-start = ((), (), s32[]{:S(2)}) async-start(), calls=%async_computation | async-start | bytes 2129920 | tf_op jit(solution)/shard_map/psum | solution.py:146
  9.6 319.7 %collective-permute-start = (s32[8]{0:T(128)S(1)}, s32[8]{0:T(128)S(1)}, u32[]{:S(2)}, u32[]{:S(2)}) collective-permute-start(s32[8]{0:T(128)S(1)} %get-tuple-element.44), channel_id=1, source_target_pairs={{0,1},{1,2},{2,3},{3,4},{4,5},{5,6},{6,7},{7,0},{8,9},{9,10},{10,1... | collective-permute-start | bytes 104 | tf_op jit(solution)/shard_map/ppermute | solution.py:13
  10.1 319.5 %collective-permute-start.1 = (s32[8]{0:T(128)S(1)}, s32[8]{0:T(128)S(1)}, u32[]{:S(2)}, u32[]{:S(2)}) collective-permute-start(s32[8]{0:T(128)S(1)} %get-tuple-element.43), channel_id=1, source_target_pairs={{0,2},{1,3},{2,4},{3,5},{4,6},{5,7},{6,0},{7,1},{8,10},{9,11},{10,... | collective-permute-start | bytes 104 | tf_op jit(solution)/shard_map/ppermute | solution.py:13
  242.8 15.9 %copy-start.5 = (bf16[8,31]{1,0:T(8,128)(2,1)S(1)}, bf16[8,31]{1,0:T(8,128)(2,1)}, u32[]{:S(2)}) copy-start(bf16[8,31]{1,0:T(8,128)(2,1)} %param.16) | copy-start | bytes 1492
  323.1 0.9 copy-start.2
  323.1 0.9 copy-start.3
  325.3 4.5 %collective-permute-start.4 = (bf16[8,16,128]{2,1,0:T(8,128)(2,1)S(1)}, bf16[8,16,128]{2,1,0:T(8,128)(2,1)S(1)}, u32[]{:S(2)}, u32[]{:S(2)}) collective-permute-start(bf16[8,16,128]{2,1,0:T(8,128)(2,1)S(1)} %get-tuple-element.35), channel_id=1, source_target_pairs={{0,1},{1,2},{2,3},{3,4},{4,5},{5,6},{6,7},{7,0},{8,9},{9,10},{10,1... | collective-permute-start | bytes 98312 | tf_op jit(solution)/shard_map/ppermute | solution.py:13
  326.6 4.8 %collective-permute-start.5 = (bf16[8,16,128]{2,1,0:T(8,128)(2,1)S(1)}, bf16[8,16,128]{2,1,0:T(8,128)(2,1)S(1)}, u32[]{:S(2)}, u32[]{:S(2)}) collective-permute-start(bf16[8,16,128]{2,1,0:T(8,128)(2,1)S(1)} %get-tuple-element.34), channel_id=1, source_target_pairs={{0,2},{1,3},{2,4},{3,5},{4,6},{5,7},{6,0},{7,1},{8,10},{9,11},{10,... | collective-permute-start | bytes 98312 | tf_op jit(solution)/shard_map/ppermute | solution.py:13
  329.2 4.5 %collective-permute-start.2 = (bf16[8,16,128]{2,1,0:T(8,128)(2,1)S(1)}, bf16[8,16,128]{2,1,0:T(8,128)(2,1)S(1)}, u32[]{:S(2)}, u32[]{:S(2)}) collective-permute-start(bf16[8,16,128]{2,1,0:T(8,128)(2,1)S(1)} %get-tuple-element.38), channel_id=1, source_target_pairs={{0,1},{1,2},{2,3},{3,4},{4,5},{5,6},{6,7},{7,0},{8,9},{9,10},{10,1... | collective-permute-start | bytes 98312 | tf_op jit(solution)/shard_map/ppermute | solution.py:13
  329.3 4.9 %collective-permute-start.3 = (bf16[8,16,128]{2,1,0:T(8,128)(2,1)S(1)}, bf16[8,16,128]{2,1,0:T(8,128)(2,1)S(1)}, u32[]{:S(2)}, u32[]{:S(2)}) collective-permute-start(bf16[8,16,128]{2,1,0:T(8,128)(2,1)S(1)} %get-tuple-element.37), channel_id=1, source_target_pairs={{0,2},{1,3},{2,4},{3,5},{4,6},{5,7},{6,0},{7,1},{8,10},{9,11},{10,... | collective-permute-start | bytes 98312 | tf_op jit(solution)/shard_map/ppermute | solution.py:13
  336.5 2.7 collective-permute-start.6
  339.2 3.1 collective-permute-start.7
  400.3 5.4 %copy-start.1 = (f32[2,1040,128]{2,1,0:T(8,128)S(1)}, f32[2,1040,128]{2,1,0:T(8,128)}, u32[]{:S(2)}) copy-start(f32[2,1040,128]{2,1,0:T(8,128)} %all-reduce.3.cloned.1.call-done) | copy-start | bytes 3194884
  403.1 3.7 collective-permute-start.8
  405.1 3.9 collective-permute-start.9
Sparse Core Ops, SparseCore 0:
  343.5 56.7 all-reduce.2
where the time goes:
time: 418 us; the launch traced here: 417 us
  local copies, waits for them, and re-layouts  317 us (76%)
  waiting for transfers between devices  63.8 us (15%)
  between operations  14.4 us (3%)
  starting transfers between devices  11.9 us (3%)
  other arithmetic  9.12 us (2%)
    gather x4, local copies, waits for them, and re-layouts, toeplitz(): band_table = jnp.take(kernel_taps, tap_index, axis=1)  309 us
    psum x1, waiting for transfers between devices, body(): totals = lax.psum(extended, 'exp')  56.9 us
    ppermute x8, starting transfers between devices, shifted(): lax.ppermute(shard, axis, [(i, (i + by) % length) for i in range(length)])  8.77 us
  transfers between devices with their start and end apart: 11, of which 7 were waited for; matrix products, arithmetic and copies ran while one was open for 76% of the time, Pallas kernels for 0%

commit v1 on v0

--- a/solution.py
+++ b/solution.py
@@ -1,3 +1,4 @@
+import functools
 import jax
 import jax.numpy as jnp
 from jax import lax
@@ -6,6 +7,15 @@
 PR = 16
 PC = 128
 TR = 1024
+
+
+def _run_views(xin, device_axis):
+    u1 = jax.lax.all_gather(xin, device_axis)
+    opened = jnp.sum(u1, 0)
+    return opened
+
+
+surface_register = functools.partial(_run_views, device_axis="exp")
 
 
 def shifted(shard, axis, by):
@@ -143,7 +153,7 @@
     core_rows = core_rows.at[:, :rim_rows].add(padded[:, :rim_rows])
     core_rows = core_rows.at[:, TR : TR + rim_rows].add(padded[:, rim_rows + extent - 1 :])
     extended = jnp.concatenate([core_rows, jnp.zeros((2, 1, PC), jnp.float32)], axis=1)
-    totals = lax.psum(extended, "exp")
+    totals = surface_register(extended)
     template_ext = (totals[0] / jnp.maximum(totals[1], 1.0)).astype(jnp.bfloat16)
     cutout = template_ext[sky_row].reshape(reach, slot_count, PR, PC)
     returned_list = [cutout[0]]

time: 418 us -> 446 us (1.067)
  waiting for transfers between devices: 63.8 us -> 92.8 us
    all_gather x0 -> x1, waiting for transfers between devices: none -> 86 us  [_run_views(): u1 = jax.lax.all_gather(xin, device_axis)]
    psum x1 -> x0, waiting for transfers between devices: 56.9 us -> none  [body(): totals = lax.psum(extended, 'exp')]
  transfers between devices with their start and end apart: 11 -> 11, of which waited for: 7 -> 7; matrix products, arithmetic and copies ran while one was open for 76% -> 71% of each run, Pallas kernels for 0% -> 0%
where the time goes in v1:
time: 446 us; the launch traced here: 445 us
  local copies, waits for them, and re-layouts  315 us (71%)
  waiting for transfers between devices  92.8 us (21%)
  between operations  14.4 us (3%)
  starting transfers between devices  11.9 us (3%)
  other arithmetic  10.4 us (2%)
    gather x4, local copies, waits for them, and re-layouts, toeplitz(): band_table = jnp.take(kernel_taps, tap_index, axis=1)  307 us
    all_gather x1, waiting for transfers between devices, _run_views(): u1 = jax.lax.all_gather(xin, device_axis)  86 us
  transfers between devices with their start and end apart: 11, of which 7 were waited for; matrix products, arithmetic and copies ran while one was open for 71% of the time, Pallas kernels for 0%

profile of v1, /device:TPU:0, one launch (start us, length us, event | category | flops | bytes accessed | tf_op | source)
XLA Modules:
  0.0 445.4 jit_solution(11665477547122041004)
XLA Ops:
  7.2 0.7 bitcast_select_fusion
  8.0 0.2 select_reduce_fusion
  8.2 0.7 fusion.64
  8.9 0.6 scatter_custom_fusion
  9.6 0.5 collective-permute-start
  10.1 2.5 collective-permute-start.1
  12.6 0.1 fusion.32
  12.9 0.7 copy.33
  13.6 0.1 copy.31
  13.8 0.1 copy.25
  13.9 227.3 %gather_fusion.1 = bf16[65536,8]{1,0:T(8,128)(2,1)} fusion(bf16[8,31]{0,1:T(8,128)(2,1)S(1)} %copy.25, s32[65536]{0:T(1024)S(1)} %broadcast_clamp_fusion), kind=kCustom, calls=%fused_computation.1 | custom fusion | bytes 2359296 | tf_op jit(solution)/shard_map/jit(_take)/gather | solution.py:49
  241.2 15.9 %copy.26 = bf16[256,256,8]{0,1,2:T(8,128)(2,1)S(1)} copy(bf16[256,256,8]{2,1,0:T(8,128)(2,1)} %bitcast.93) | data formatting | bytes 2097152 | tf_op jit(solution)/shard_map/jit(_take)/gather | solution.py:49
  257.1 0.1 copy.23
  257.2 57.4 %gather_fusion = bf16[16384,8]{1,0:T(8,128)(2,1)} fusion(bf16[8,31]{0,1:T(8,128)(2,1)S(1)} %copy.23, s32[16384]{0:T(1024)S(1)} %fusion.44), kind=kCustom, calls=%fused_computation | custom fusion | bytes 589824 | tf_op jit(solution)/shard_map/jit(_take)/gather | solution.py:49
  314.6 6.3 %copy.24 = bf16[128,128,8]{0,1,2:T(8,128)(2,1)S(1)} copy(bf16[128,128,8]{2,1,0:T(8,128)(2,1)} %bitcast.100) | data formatting | bytes 524288 | tf_op jit(solution)/shard_map/jit(_take)/gather | solution.py:49
  321.1 0.8 fusion
  322.1 0.1 convert_bitcast_fusion.1
  322.2 1.0 scatter_fusion.1
  323.3 1.3 collective-permute-start.4
  324.6 1.5 collective-permute-start.5
  326.1 1.0 scatter_fusion
  327.2 0.1 collective-permute-start.2
  327.3 0.3 collective-permute-start.3
  327.6 0.1 add_select_fusion
  327.7 0.1 select_n.155
  327.8 1.6 collective-permute-done.5
  329.4 2.3 scatter_custom_fusion.4
  331.7 0.4 collective-permute-done.3
  332.2 2.3 scatter_custom_fusion.2
  334.5 1.8 collective-permute-start.6
  336.3 0.8 collective-permute-done.6
  337.2 1.3 collective-permute-start.7
  338.5 0.2 scatter-add.26
  338.7 1.5 collective-permute-done.7
  340.2 1.0 concatenate.11
  341.3 86.0 %all-gather.3.cloned.1.call-done = f32[8,1040,128]{2,1,0:T(8,128)} async-done(((f32[2,1040,128]{2,1,0:T(8,128)}), f32[8,1040,128]{2,1,0:T(8,128)}) %all-gather.3.cloned.1.call-update) | async-done | bytes 4259856 | tf_op jit(solution)/shard_map/all_gather | solution.py:13
  427.3 2.5 reduce_sum.37
  429.9 0.1 fusion.74
  429.9 0.1 fusion.13
  430.0 1.4 gather_fusion.2
  431.5 1.7 collective-permute-start.8
  433.2 0.8 collective-permute-start.9
  434.0 0.7 slice_bitcast_fusion
  434.7 0.1 collective-permute-done.8
  434.8 2.3 collective-permute-done.9
  437.2 0.6 gather_fusion.3
  437.8 0.1 reshape.546
  438.0 0.6 fusion.39
  (52 shorter events, 1.1 us)
Async XLA Ops:
  7.2 313.9 %copy-start = (bf16[1,1,128,256]{3,2,1,0:T(8,128)(2,1)S(1)}, bf16[1,1,128,256]{3,2,1,0:T(8,128)(2,1)}, u32[]{:S(2)}) copy-start(bf16[1,1,128,256]{3,2,1,0:T(8,128)(2,1)} %param.12) | copy-start | bytes 196612
  7.2 6.6 %copy-start.3 = (bf16[8,31]{1,0:T(8,128)(2,1)S(1)}, bf16[8,31]{1,0:T(8,128)(2,1)}, u32[]{:S(2)}) copy-start(bf16[8,31]{1,0:T(8,128)(2,1)} %param.17) | copy-start | bytes 1492
  7.2 420.1 %all-gather.3.cloned.1.call-start = ((), (), s32[]{:S(2)}) async-start(), calls=%async_computation | async-start | bytes 5324800 | tf_op jit(solution)/shard_map/all_gather | solution.py:13
  9.6 317.7 %collective-permute-start = (s32[8]{0:T(128)S(1)}, s32[8]{0:T(128)S(1)}, u32[]{:S(2)}, u32[]{:S(2)}) collective-permute-start(s32[8]{0:T(128)S(1)} %get-tuple-element.44), channel_id=1, source_target_pairs={{0,1},{1,2},{2,3},{3,4},{4,5},{5,6},{6,7},{7,0},{8,9},{9,10},{10,1... | collective-permute-start | bytes 104 | tf_op jit(solution)/shard_map/ppermute | solution.py:23
  10.1 317.5 %collective-permute-start.1 = (s32[8]{0:T(128)S(1)}, s32[8]{0:T(128)S(1)}, u32[]{:S(2)}, u32[]{:S(2)}) collective-permute-start(s32[8]{0:T(128)S(1)} %get-tuple-element.43), channel_id=1, source_target_pairs={{0,2},{1,3},{2,4},{3,5},{4,6},{5,7},{6,0},{7,1},{8,10},{9,11},{10,... | collective-permute-start | bytes 104 | tf_op jit(solution)/shard_map/ppermute | solution.py:23
  241.2 15.9 %copy-start.4 = (bf16[8,31]{1,0:T(8,128)(2,1)S(1)}, bf16[8,31]{1,0:T(8,128)(2,1)}, u32[]{:S(2)}) copy-start(bf16[8,31]{1,0:T(8,128)(2,1)} %param.16) | copy-start | bytes 1492
  321.1 0.9 copy-start.1
  321.1 0.9 copy-start.2
  323.3 4.5 %collective-permute-start.4 = (bf16[8,16,128]{2,1,0:T(8,128)(2,1)S(1)}, bf16[8,16,128]{2,1,0:T(8,128)(2,1)S(1)}, u32[]{:S(2)}, u32[]{:S(2)}) collective-permute-start(bf16[8,16,128]{2,1,0:T(8,128)(2,1)S(1)} %get-tuple-element.35), channel_id=1, source_target_pairs={{0,1},{1,2},{2,3},{3,4},{4,5},{5,6},{6,7},{7,0},{8,9},{9,10},{10,1... | collective-permute-start | bytes 98312 | tf_op jit(solution)/shard_map/ppermute | solution.py:23
  324.6 4.8 %collective-permute-start.5 = (bf16[8,16,128]{2,1,0:T(8,128)(2,1)S(1)}, bf16[8,16,128]{2,1,0:T(8,128)(2,1)S(1)}, u32[]{:S(2)}, u32[]{:S(2)}) collective-permute-start(bf16[8,16,128]{2,1,0:T(8,128)(2,1)S(1)} %get-tuple-element.34), channel_id=1, source_target_pairs={{0,2},{1,3},{2,4},{3,5},{4,6},{5,7},{6,0},{7,1},{8,10},{9,11},{10,... | collective-permute-start | bytes 98312 | tf_op jit(solution)/shard_map/ppermute | solution.py:23
  327.2 4.5 %collective-permute-start.2 = (bf16[8,16,128]{2,1,0:T(8,128)(2,1)S(1)}, bf16[8,16,128]{2,1,0:T(8,128)(2,1)S(1)}, u32[]{:S(2)}, u32[]{:S(2)}) collective-permute-start(bf16[8,16,128]{2,1,0:T(8,128)(2,1)S(1)} %get-tuple-element.38), channel_id=1, source_target_pairs={{0,1},{1,2},{2,3},{3,4},{4,5},{5,6},{6,7},{7,0},{8,9},{9,10},{10,1... | collective-permute-start | bytes 98312 | tf_op jit(solution)/shard_map/ppermute | solution.py:23
  327.3 4.9 %collective-permute-start.3 = (bf16[8,16,128]{2,1,0:T(8,128)(2,1)S(1)}, bf16[8,16,128]{2,1,0:T(8,128)(2,1)S(1)}, u32[]{:S(2)}, u32[]{:S(2)}) collective-permute-start(bf16[8,16,128]{2,1,0:T(8,128)(2,1)S(1)} %get-tuple-element.37), channel_id=1, source_target_pairs={{0,2},{1,3},{2,4},{3,5},{4,6},{5,7},{6,0},{7,1},{8,10},{9,11},{10,... | collective-permute-start | bytes 98312 | tf_op jit(solution)/shard_map/ppermute | solution.py:23
  334.5 2.7 collective-permute-start.6
  337.2 3.1 collective-permute-start.7
  431.5 3.3 collective-permute-start.8
  433.2 3.9 collective-permute-start.9
Sparse Core Ops, SparseCore 0:
  341.4 85.8 all-gather.2
